TPU v7x, 256 devices: a whole 4x4x8 slice. The times are simulated.
256 devices in a mesh: panel: 8 (over x, core), front: 32 (over z, y).
Axes of the slice: x: 4, y: 4, z: 8, core: 2. Of those that a mesh axis runs over, the one named last changes fastest.
Arguments:
- rhs: float32 [8, 64, 64, 2, 128], P('panel', None, 'front'), may hold values from -6 to 6
- fronts: bfloat16 [8, 2, 8192, 8192], P('panel', None, 'front'), may hold values from -0.046875 to 0.046875
- wave_sq: float32 [8, 64, 128], P('panel', 'front'), may hold values from 0.5 to 2
- pml_width: int32 [8], P('panel'), may hold values from 1 to 16
Outputs:
- sweep_field: float32 [8, 64, 64, 2, 128], P('panel', None, 'front')
- residual: float32 [8, 64, 64, 2, 128], P('panel', None, 'front')
All inputs are finite; a program needn't handle non-finite values.
Results may differ from a plain program's by a relative error of at most 0.013.
Values may be sent and summed in bfloat16 or wider, within the bound.
A program may use at most 64 MiB of HBM per device.

v0:
```python
import jax
import jax.numpy as jnp
from jax import lax
from jax.sharding import PartitionSpec as P


def from_behind(shard, axis, by):
    devices = lax.axis_size(axis)
    pairs = [(i, i + by) for i in range(devices) if 0 <= i + by < devices]
    return lax.ppermute(shard, axis, pairs)


def padded_2(cells, sides, width):
    for axis, dim in sides:
        count = lax.axis_size(axis)
        ends = count - 1
        head = lax.slice_in_dim(cells, 0, width, axis=dim)
        tail = lax.slice_in_dim(cells, cells.shape[dim] - width, cells.shape[dim], axis=dim)
        cells = jnp.concatenate(
            [
                lax.ppermute(tail, axis, [(i, (i + 1) % count) for i in range(ends)]),
                cells,
                lax.ppermute(head, axis, [((i + 1) % count, i) for i in range(ends)]),
            ],
            axis=dim,
        )
    return cells


def local(rhs, fronts, wave_sq, pml_width):
    group_panels, rhs_count, row_count, components, columns = rhs.shape
    panel_count = lax.axis_size("panel")
    group_index = lax.axis_index("panel")
    block_count = 1
    block_size = rhs_count // block_count

    def apply_front(combined, local_panel):
        front_re = fronts[local_panel, 0]
        front_im = fronts[local_panel, 1]
        vector_piece = lax.all_gather(combined, "front", axis=1, tiled=True)
        piece_rows = vector_piece.shape[1]
        width = piece_rows * columns
        part_re = vector_piece[:, :, 0].reshape(block_size, width)
        part_im = vector_piece[:, :, 1].reshape(block_size, width)
        dims = (((1,), (1,)), ((), ()))
        new_re = lax.dot_general(
            part_re, front_re, dims, preferred_element_type=jnp.float32
        ) - lax.dot_general(part_im, front_im, dims, preferred_element_type=jnp.float32)
        new_im = lax.dot_general(
            part_re, front_im, dims, preferred_element_type=jnp.float32
        ) + lax.dot_general(part_im, front_re, dims, preferred_element_type=jnp.float32)
        return jnp.stack(
            [
                new_re.reshape(block_size, row_count, columns),
                new_im.reshape(block_size, row_count, columns),
            ],
            axis=2,
        )

    def one_section(section_num, carry):
        solved_all, incoming = carry
        block_num = section_num - group_index
        active = (block_num >= 0) & (block_num < block_count)
        previous = incoming
        rhs_block = rhs[0]
        combined = (rhs_block + previous).astype(jnp.bfloat16)
        solved = apply_front(combined, 0)
        earlier = solved_all
        solved_all = jnp.where(active, solved[None], earlier)
        incoming = from_behind(solved, "panel", 1)
        return (solved_all, incoming)

    start_all = jnp.zeros(rhs.shape, jnp.float32)
    start_in = jnp.zeros((block_size, row_count, components, columns), jnp.float32)
    sweep_field, _ = lax.fori_loop(
        0, panel_count + block_count - 1, one_section, (start_all, start_in)
    )
    padded = padded_2(sweep_field.astype(jnp.bfloat16), (("panel", 0), ("front", 2)), 1).astype(
        sweep_field.dtype
    )
    beside = padded[2:, :, 1:-1] + padded[:-2, :, 1:-1]
    beside = beside + padded[1:-1, :, 2:] + padded[1:-1, :, :-2]
    side_pad = jnp.pad(sweep_field, ((0, 0), (0, 0), (0, 0), (0, 0), (1, 1)))
    beside = beside + side_pad[..., 2:] + side_pad[..., :-2]
    plane_rows = lax.axis_index("front") * row_count + jnp.arange(row_count, dtype=jnp.int32)
    row_pos = plane_rows.astype(jnp.float32)[None, :]
    total_rows = row_count * lax.axis_size("front")
    thick = pml_width.astype(jnp.float32)[:, None]
    absorb = (
        2.0
        * (jnp.maximum(0.0, thick - row_pos) + jnp.maximum(0.0, row_pos - (total_rows - 1 - thick)))
        / thick
    )
    absorb_b = absorb[:, None, :, None]
    diagonal_term = (6.0 - wave_sq)[:, None, :, :]
    real_part = sweep_field[:, :, :, 0]
    imag_part = sweep_field[:, :, :, 1]
    apply_re = diagonal_term * real_part - absorb_b * imag_part - beside[:, :, :, 0]
    apply_im = diagonal_term * imag_part + absorb_b * real_part - beside[:, :, :, 1]
    residual = rhs - jnp.stack([apply_re, apply_im], axis=3)
    return (sweep_field, residual)


def solution(mesh):
    return jax.shard_map(
        local,
        mesh=mesh,
        in_specs=(
            P("panel", None, "front", None, None),
            P("panel", None, "front", None),
            P("panel", "front", None),
            P("panel"),
        ),
        out_specs=(P("panel", None, "front", None, None), P("panel", None, "front", None, None)),
        check_vma=False,
    )
```

profile of v0, /device:TPU:29, one launch (start us, length us, event | category | flops | bytes accessed | tf_op | source)
XLA Modules:
  0.0 821.7 jit_solution(15315599184756848549)
XLA Ops:
  8.2 782.1 %while.16 = (s32[]{:T(128)}, f32[1,64,2,2,128]{4,2,1,3,0:T(2,128)S(1)}, f32[64,2,2,128]{3,1,0,2:T(2,128)S(1)}, s32[]{:T(128)}, f32[1,64,2,2,128]{4,1,3,2,0:T(8,1...) while((s32[]{:T(128)}, f32[1,64,2,2,128]{4,2,1,3,0:T(2,128)S(1)}, ...), condition=%wide.region_1.2_spmd.clone, body=%wide.region_0.1_spmd.clone.sunk | while | flops 1073905664 | bytes 71565536 | solution.py:75
  8.9 78.8 %all-gather.2.cloned.1.call-done = bf16[64,64,2,128]{3,0,2,1:T(8,128)(2,1)} async-done(((bf16[64,2,2,128]{3,0,2,1:T(8,128)(2,1)}), bf16[64,64,2,128]{3,0,2,1:T(8,128)(2,1)}) %all-gather.2.cloned.1.call-update) | async-done | bytes 2097168 | tf_op jit(solution)/shard_map/while/body/eval_jaxpr/all_gather | solution.py:40
  96.0 3.7 fusion.58
  99.8 7.0 collective-permute-start
  109.4 75.8 %all-gather.2.cloned.1.call-done = bf16[64,64,2,128]{3,0,2,1:T(8,128)(2,1)} async-done(((bf16[64,2,2,128]{3,0,2,1:T(8,128)(2,1)}), bf16[64,64,2,128]{3,0,2,1:T(8,128)(2,1)}) %all-gather.2.cloned.1.call-update) | async-done | bytes 2097168 | tf_op jit(solution)/shard_map/while/body/eval_jaxpr/all_gather | solution.py:40
  193.5 3.7 fusion.58
  197.3 7.0 collective-permute-start
  206.9 75.8 %all-gather.2.cloned.1.call-done = bf16[64,64,2,128]{3,0,2,1:T(8,128)(2,1)} async-done(((bf16[64,2,2,128]{3,0,2,1:T(8,128)(2,1)}), bf16[64,64,2,128]{3,0,2,1:T(8,128)(2,1)}) %all-gather.2.cloned.1.call-update) | async-done | bytes 2097168 | tf_op jit(solution)/shard_map/while/body/eval_jaxpr/all_gather | solution.py:40
  294.8 7.0 collective-permute-start
  304.4 75.5 %all-gather.2.cloned.1.call-done = bf16[64,64,2,128]{3,0,2,1:T(8,128)(2,1)} async-done(((bf16[64,2,2,128]{3,0,2,1:T(8,128)(2,1)}), bf16[64,64,2,128]{3,0,2,1:T(8,128)(2,1)}) %all-gather.2.cloned.1.call-update) | async-done | bytes 2097168 | tf_op jit(solution)/shard_map/while/body/eval_jaxpr/all_gather | solution.py:40
  388.2 3.7 fusion.58
  391.9 7.0 collective-permute-start
  401.6 75.5 %all-gather.2.cloned.1.call-done = bf16[64,64,2,128]{3,0,2,1:T(8,128)(2,1)} async-done(((bf16[64,2,2,128]{3,0,2,1:T(8,128)(2,1)}), bf16[64,64,2,128]{3,0,2,1:T(8,128)(2,1)}) %all-gather.2.cloned.1.call-update) | async-done | bytes 2097168 | tf_op jit(solution)/shard_map/while/body/eval_jaxpr/all_gather | solution.py:40
  485.4 3.7 fusion.58
  489.1 7.0 collective-permute-start
  498.7 75.5 %all-gather.2.cloned.1.call-done = bf16[64,64,2,128]{3,0,2,1:T(8,128)(2,1)} async-done(((bf16[64,2,2,128]{3,0,2,1:T(8,128)(2,1)}), bf16[64,64,2,128]{3,0,2,1:T(8,128)(2,1)}) %all-gather.2.cloned.1.call-update) | async-done | bytes 2097168 | tf_op jit(solution)/shard_map/while/body/eval_jaxpr/all_gather | solution.py:40
  586.3 7.0 collective-permute-start
  596.0 75.8 %all-gather.2.cloned.1.call-done = bf16[64,64,2,128]{3,0,2,1:T(8,128)(2,1)} async-done(((bf16[64,2,2,128]{3,0,2,1:T(8,128)(2,1)}), bf16[64,64,2,128]{3,0,2,1:T(8,128)(2,1)}) %all-gather.2.cloned.1.call-update) | async-done | bytes 2097168 | tf_op jit(solution)/shard_map/while/body/eval_jaxpr/all_gather | solution.py:40
  683.8 7.0 collective-permute-start
  693.5 75.8 %all-gather.2.cloned.1.call-done = bf16[64,64,2,128]{3,0,2,1:T(8,128)(2,1)} async-done(((bf16[64,2,2,128]{3,0,2,1:T(8,128)(2,1)}), bf16[64,64,2,128]{3,0,2,1:T(8,128)(2,1)}) %all-gather.2.cloned.1.call-update) | async-done | bytes 2097168 | tf_op jit(solution)/shard_map/while/body/eval_jaxpr/all_gather | solution.py:40
  781.3 7.0 collective-permute-start
  790.4 4.4 collective-permute-start.1
  800.8 3.8 collective-permute-start.3
  806.9 6.4 collective-permute-done.4
  (162 shorter events, 112.6 us)
Async XLA Ops:
  8.1 788.5 %copy-start.2 = (f32[1,2,128]{2,1,0:T(2,128)S(1)}, f32[1,2,128]{2,1,0:T(2,128)}, u32[]{:S(2)}) copy-start(f32[1,2,128]{2,1,0:T(2,128)} %param.8) | copy-start | bytes 3076
  8.2 805.9 %copy-start.1 = (f32[1,64,2,2,128]{4,3,2,1,0:T(2,128)S(1)}, f32[1,64,2,2,128]{4,3,2,1,0:T(2,128)}, u32[]{:S(2)}) copy-start(f32[1,64,2,2,128]{4,3,2,1,0:T(2,128)} %param.6) | copy-start | bytes 393220
  8.2 79.5 %all-gather.2.cloned.1.call-start = ((), (), s32[]{:S(2)}) async-start(), calls=%async_computation | async-start | bytes 2162688 | tf_op jit(solution)/shard_map/while/body/eval_jaxpr/all_gather | solution.py:40
  99.8 8.9 %collective-permute-start = (f32[64,2,2,128]{3,1,0,2:T(2,128)S(1)}, f32[64,2,2,128]{3,1,0,2:T(2,128)S(1)}, u32[]{:S(2)}, u32[]{:S(2)}) collective-permute-start(f32[64,2,2,128]{3,1,0,2:T(2,128)S(1)} %constant_dynamic-update-slice_fusion.5), channel_id=1, source_target_pairs={{0,32},{32,64},{64,96},{96,128},{128,160},{160,192},{192,224},{1,3... | collective-permute-start | bytes 393224 | tf_op jit(solution)/shard_map/while/body/eval_jaxpr/ppermute | solution.py:10
  108.7 76.5 %all-gather.2.cloned.1.call-start = ((), (), s32[]{:S(2)}) async-start(), calls=%async_computation | async-start | bytes 2162688 | tf_op jit(solution)/shard_map/while/body/eval_jaxpr/all_gather | solution.py:40
  185.2 4.0 copy-start.3
  197.3 8.9 %collective-permute-start = (f32[64,2,2,128]{3,1,0,2:T(2,128)S(1)}, f32[64,2,2,128]{3,1,0,2:T(2,128)S(1)}, u32[]{:S(2)}, u32[]{:S(2)}) collective-permute-start(f32[64,2,2,128]{3,1,0,2:T(2,128)S(1)} %constant_dynamic-update-slice_fusion.5), channel_id=1, source_target_pairs={{0,32},{32,64},{64,96},{96,128},{128,160},{160,192},{192,224},{1,3... | collective-permute-start | bytes 393224 | tf_op jit(solution)/shard_map/while/body/eval_jaxpr/ppermute | solution.py:10
  206.2 76.5 %all-gather.2.cloned.1.call-start = ((), (), s32[]{:S(2)}) async-start(), calls=%async_computation | async-start | bytes 2162688 | tf_op jit(solution)/shard_map/while/body/eval_jaxpr/all_gather | solution.py:40
  294.8 8.9 %collective-permute-start = (f32[64,2,2,128]{3,1,0,2:T(2,128)S(1)}, f32[64,2,2,128]{3,1,0,2:T(2,128)S(1)}, u32[]{:S(2)}, u32[]{:S(2)}) collective-permute-start(f32[64,2,2,128]{3,1,0,2:T(2,128)S(1)} %constant_dynamic-update-slice_fusion.5), channel_id=1, source_target_pairs={{0,32},{32,64},{64,96},{96,128},{128,160},{160,192},{192,224},{1,3... | collective-permute-start | bytes 393224 | tf_op jit(solution)/shard_map/while/body/eval_jaxpr/ppermute | solution.py:10
  303.7 76.2 %all-gather.2.cloned.1.call-start = ((), (), s32[]{:S(2)}) async-start(), calls=%async_computation | async-start | bytes 2162688 | tf_op jit(solution)/shard_map/while/body/eval_jaxpr/all_gather | solution.py:40
  391.9 8.9 %collective-permute-start = (f32[64,2,2,128]{3,1,0,2:T(2,128)S(1)}, f32[64,2,2,128]{3,1,0,2:T(2,128)S(1)}, u32[]{:S(2)}, u32[]{:S(2)}) collective-permute-start(f32[64,2,2,128]{3,1,0,2:T(2,128)S(1)} %constant_dynamic-update-slice_fusion.5), channel_id=1, source_target_pairs={{0,32},{32,64},{64,96},{96,128},{128,160},{160,192},{192,224},{1,3... | collective-permute-start | bytes 393224 | tf_op jit(solution)/shard_map/while/body/eval_jaxpr/ppermute | solution.py:10
  400.9 76.2 %all-gather.2.cloned.1.call-start = ((), (), s32[]{:S(2)}) async-start(), calls=%async_computation | async-start | bytes 2162688 | tf_op jit(solution)/shard_map/while/body/eval_jaxpr/all_gather | solution.py:40
  489.1 8.9 %collective-permute-start = (f32[64,2,2,128]{3,1,0,2:T(2,128)S(1)}, f32[64,2,2,128]{3,1,0,2:T(2,128)S(1)}, u32[]{:S(2)}, u32[]{:S(2)}) collective-permute-start(f32[64,2,2,128]{3,1,0,2:T(2,128)S(1)} %constant_dynamic-update-slice_fusion.5), channel_id=1, source_target_pairs={{0,32},{32,64},{64,96},{96,128},{128,160},{160,192},{192,224},{1,3... | collective-permute-start | bytes 393224 | tf_op jit(solution)/shard_map/while/body/eval_jaxpr/ppermute | solution.py:10
  498.1 76.2 %all-gather.2.cloned.1.call-start = ((), (), s32[]{:S(2)}) async-start(), calls=%async_computation | async-start | bytes 2162688 | tf_op jit(solution)/shard_map/while/body/eval_jaxpr/all_gather | solution.py:40
  586.3 8.9 %collective-permute-start = (f32[64,2,2,128]{3,1,0,2:T(2,128)S(1)}, f32[64,2,2,128]{3,1,0,2:T(2,128)S(1)}, u32[]{:S(2)}, u32[]{:S(2)}) collective-permute-start(f32[64,2,2,128]{3,1,0,2:T(2,128)S(1)} %constant_dynamic-update-slice_fusion.5), channel_id=1, source_target_pairs={{0,32},{32,64},{64,96},{96,128},{128,160},{160,192},{192,224},{1,3... | collective-permute-start | bytes 393224 | tf_op jit(solution)/shard_map/while/body/eval_jaxpr/ppermute | solution.py:10
  595.2 76.5 %all-gather.2.cloned.1.call-start = ((), (), s32[]{:S(2)}) async-start(), calls=%async_computation | async-start | bytes 2162688 | tf_op jit(solution)/shard_map/while/body/eval_jaxpr/all_gather | solution.py:40
  683.8 8.9 %collective-permute-start = (f32[64,2,2,128]{3,1,0,2:T(2,128)S(1)}, f32[64,2,2,128]{3,1,0,2:T(2,128)S(1)}, u32[]{:S(2)}, u32[]{:S(2)}) collective-permute-start(f32[64,2,2,128]{3,1,0,2:T(2,128)S(1)} %constant_dynamic-update-slice_fusion.5), channel_id=1, source_target_pairs={{0,32},{32,64},{64,96},{96,128},{128,160},{160,192},{192,224},{1,3... | collective-permute-start | bytes 393224 | tf_op jit(solution)/shard_map/while/body/eval_jaxpr/ppermute | solution.py:10
  692.7 76.5 %all-gather.2.cloned.1.call-start = ((), (), s32[]{:S(2)}) async-start(), calls=%async_computation | async-start | bytes 2162688 | tf_op jit(solution)/shard_map/while/body/eval_jaxpr/all_gather | solution.py:40
  781.3 8.9 %collective-permute-start = (f32[64,2,2,128]{3,1,0,2:T(2,128)S(1)}, f32[64,2,2,128]{3,1,0,2:T(2,128)S(1)}, u32[]{:S(2)}, u32[]{:S(2)}) collective-permute-start(f32[64,2,2,128]{3,1,0,2:T(2,128)S(1)} %constant_dynamic-update-slice_fusion.5), channel_id=1, source_target_pairs={{0,32},{32,64},{64,96},{96,128},{128,160},{160,192},{192,224},{1,3... | collective-permute-start | bytes 393224 | tf_op jit(solution)/shard_map/while/body/eval_jaxpr/ppermute | solution.py:10
  790.4 24.5 %copy-start = (f32[1,64,2,2,128]{4,3,2,1,0:T(2,128)}, f32[1,64,2,2,128]{4,3,2,1,0:T(2,128)S(1)}, u32[]{:S(2)}) copy-start(f32[1,64,2,2,128]{4,3,2,1,0:T(2,128)S(1)} %get-tuple-element.170) | copy-start | bytes 393220
  790.4 7.0 collective-permute-start.1
  794.8 5.6 collective-permute-start.2
  800.8 6.1 collective-permute-start.3
  804.6 8.7 %collective-permute-start.4 = (bf16[3,64,1,2,128]{4,3,2,1,0:T(2,128)(2,1)S(1)}, bf16[3,64,1,2,128]{4,3,2,1,0:T(2,128)(2,1)S(1)}, u32[]{:S(2)}, u32[]{:S(2)}) collective-permute-start(bf16[3,64,1,2,128]{4,3,2,1,0:T(2,128)(2,1)S(1)} %get-tuple-element.176), channel_id=1, source_target_pairs={{1,0},{2,1},{3,2},{4,3},{5,4},{6,5},{7,6},{8,7},{9,8},{10,9},{11,1... | collective-permute-start | bytes 294920 | tf_op jit(solution)/shard_map/ppermute | solution.py:23
  (7 other events, 28.1 us)
Sparse Core Ops, SparseCore 0:
  12.2 75.4 all-gather.1
  112.7 72.5 all-gather.1
  210.2 72.5 all-gather.1
  307.3 72.5 all-gather.1
  404.5 72.5 all-gather.1
  501.7 72.5 all-gather.1
  599.2 72.5 all-gather.1
  696.7 72.5 all-gather.1
where the time goes:
time: 822 us
  waiting for transfers between devices  633 us (77%)
  starting transfers between devices  67.9 us (8%)
  matrix products  63.2 us (8%)
  local copies, waits for them, and re-layouts  33.8 us (4%)
  between operations  14.8 us (2%)
  other arithmetic  8.63 us (1%)
    all_gather x8, waiting for transfers between devices, apply_front(): vector_piece = lax.all_gather(combined, 'front', axis=1, tiled=True)  609 us
    ppermute x8, starting transfers between devices, from_behind(): return lax.ppermute(shard, axis, pairs)  55.9 us
    dot_general x8, matrix products, apply_front(): lax.dot_general(part_re, front_re, dims, preferred_element_type=jnp.float32)  29.3 us
    slice x16, local copies, waits for them, and re-layouts, apply_front(): part_re = vector_piece[:, :, 0].reshape(block_size, width)  20.5 us
  transfers between devices with their start and end apart: 20, of which 19 were waited for; matrix products, arithmetic and copies ran while one was open for 0% of the time, Pallas kernels for 0%

commit v1 on v0

--- a/solution.py
+++ b/solution.py
@@ -37,7 +37,8 @@
     def apply_front(combined, local_panel):
         front_re = fronts[local_panel, 0]
         front_im = fronts[local_panel, 1]
-        vector_piece = lax.all_gather(combined, "front", axis=1, tiled=True)
+        sent = jnp.stack([combined] * lax.axis_size("front"))
+        vector_piece = jnp.concatenate(lax.all_to_all(sent, "front", 0, 0), axis=1)
         piece_rows = vector_piece.shape[1]
         width = piece_rows * columns
         part_re = vector_piece[:, :, 0].reshape(block_size, width)

time: 822 us -> 621 us (0.76)
  waiting for transfers between devices: 633 us -> 394 us
  starting transfers between devices: 67.9 us -> 108 us
  between operations: 14.8 us -> 1.42 us
  local copies, waits for them, and re-layouts: 33.8 us -> 43.8 us
    all_gather x8 -> x0, waiting for transfers between devices: 609 us -> none  [apply_front(): vector_piece = lax.all_gather(combined, 'front', axis=1, tiled=True)]
    all_to_all x0 -> x8, waiting for transfers between devices: none -> 372 us  [apply_front(): vector_piece = jnp.concatenate(lax.all_to_all(sent, 'front', 0, 0), axis=1)]
    all_to_all x0 -> x8, starting transfers between devices: none -> 50.1 us  [apply_front(): vector_piece = jnp.concatenate(lax.all_to_all(sent, 'front', 0, 0), axis=1)]
    another operation x0 -> x8, local copies, waits for them, and re-layouts: none -> 14.9 us  [apply_front(): sent = jnp.stack([combined] * lax.axis_size('front'))]
    slice x16, local copies, waits for them, and re-layouts: 20.5 us -> 6.81 us  [apply_front(): part_re = vector_piece[:, :, 0].reshape(block_size, width)]
    ppermute x8, starting transfers between devices: 55.9 us -> 44.7 us  [from_behind(): return lax.ppermute(shard, axis, pairs)]
    while x24, local copies, waits for them, and re-layouts: 6.14 us -> 14.7 us
  transfers between devices with their start and end apart: 20 -> 20, of which waited for: 19 -> 18; matrix products, arithmetic and copies ran while one was open for 0% -> 0% of each run, Pallas kernels for 0% -> 0%
where the time goes in v1:
time: 621 us; the launch traced here: 615 us
  waiting for transfers between devices  394 us (63%)
  starting transfers between devices  108 us (17%)
  matrix products  63.2 us (10%)
  local copies, waits for them, and re-layouts  43.8 us (7%)
    all_to_all x8, waiting for transfers between devices, apply_front(): vector_piece = jnp.concatenate(lax.all_to_all(sent, 'front', 0, 0), axis=1)  372 us
    all_to_all x8, starting transfers between devices, apply_front(): vector_piece = jnp.concatenate(lax.all_to_all(sent, 'front', 0, 0), axis=1)  50.1 us
    ppermute x8, starting transfers between devices, from_behind(): return lax.ppermute(shard, axis, pairs)  44.7 us
    dot_general x8, matrix products, apply_front(): lax.dot_general(part_re, front_re, dims, preferred_element_type=jnp.float32)  29.3 us
    another operation x8, local copies, waits for them, and re-layouts, apply_front(): sent = jnp.stack([combined] * lax.axis_size('front'))  14.9 us
    ppermute x8, waiting for transfers between devices, from_behind(): return lax.ppermute(shard, axis, pairs)  14.7 us
    while x24, local copies, waits for them, and re-layouts  14.7 us
  transfers between devices with their start and end apart: 20, of which 18 were waited for; matrix products, arithmetic and copies ran while one was open for 0% of the time, Pallas kernels for 0%

profile of v1, /device:TPU:29, one launch (start us, length us, event | category | flops | bytes accessed | tf_op | source)
XLA Modules:
  0.0 614.5 jit_solution(4500301320116646153)
XLA Ops:
  1.7 590.3 %while.16 = (s32[]{:T(128)}, f32[1,64,2,2,128]{4,2,1,3,0:T(2,128)S(1)}, f32[64,2,2,128]{3,1,0,2:T(2,128)S(1)}, s32[]{:T(128)}, f32[1,64,2,2,128]{4,2,1,3,0:T(2,1...) while((s32[]{:T(128)}, f32[1,64,2,2,128]{4,2,1,3,0:T(2,128)S(1)}, ...), condition=%wide.region_1.2_spmd.clone, body=%wide.region_0.1_spmd.clone.sunk | while | flops 1073905664 | bytes 73662688 | solution.py:76
  3.7 10.9 %all-to-all-start = ((bf16[32,64,2,2,128]{4,1,3,2,0:T(8,128)(2,1)}), bf16[32,64,2,2,128]{4,1,3,2,0:T(8,128)(2,1)S(1)}, u32[]{:S(2)}, u32[]{:S(2)}) async-start(bf16[32,64,2,2,128]{4,1,3,2,0:T(8,128)(2,1)} %stack.18), calls=%async_computation | async-start | bytes 4194304 | tf_op jit(solution)/shard_map/while/body/eval_jaxpr/all_to_all | solution.py:41
  14.6 50.4 %all-to-all-done = bf16[32,64,2,2,128]{4,1,3,2,0:T(8,128)(2,1)S(1)} async-done(((bf16[32,64,2,2,128]{4,1,3,2,0:T(8,128)(2,1)}), bf16[32,64,2,2,128]{4,1,3,2,0:T(8,128)(2,1)S(1)}, u32[]{:S(2)}, u32[]{:S(2)}) %all-to-all-start) | async-done | bytes 2097184 | tf_op jit(solution)/shard_map/while/body/eval_jaxpr/all_to_all | solution.py:41
  83.6 5.7 all-to-all-start
  89.4 49.2 %all-to-all-done = bf16[32,64,2,2,128]{4,1,3,2,0:T(8,128)(2,1)S(1)} async-done(((bf16[32,64,2,2,128]{4,1,3,2,0:T(8,128)(2,1)}), bf16[32,64,2,2,128]{4,1,3,2,0:T(8,128)(2,1)S(1)}, u32[]{:S(2)}, u32[]{:S(2)}) %all-to-all-start) | async-done | bytes 2097184 | tf_op jit(solution)/shard_map/while/body/eval_jaxpr/all_to_all | solution.py:41
  157.2 5.0 all-to-all-start
  162.3 45.4 %all-to-all-done = bf16[32,64,2,2,128]{4,1,3,2,0:T(8,128)(2,1)S(1)} async-done(((bf16[32,64,2,2,128]{4,1,3,2,0:T(8,128)(2,1)}), bf16[32,64,2,2,128]{4,1,3,2,0:T(8,128)(2,1)S(1)}, u32[]{:S(2)}, u32[]{:S(2)}) %all-to-all-start) | async-done | bytes 2097184 | tf_op jit(solution)/shard_map/while/body/eval_jaxpr/all_to_all | solution.py:41
  219.1 6.5 %collective-permute-start = (f32[64,2,2,128]{3,1,0,2:T(2,128)S(1)}, f32[64,2,2,128]{3,1,0,2:T(2,128)S(1)}, u32[]{:S(2)}, u32[]{:S(2)}) collective-permute-start(f32[64,2,2,128]{3,1,0,2:T(2,128)S(1)} %constant_dynamic-update-slice_fusion.5), channel_id=1, source_target_pairs={{0,32},{32,64},{64,96},{96,128},{128,160},{160,192},{192,224},{1,3... | collective-permute-start | bytes 393224 | tf_op jit(solution)/shard_map/while/body/eval_jaxpr/ppermute | solution.py:10
  229.5 5.7 all-to-all-start
  235.2 45.4 %all-to-all-done = bf16[32,64,2,2,128]{4,1,3,2,0:T(8,128)(2,1)S(1)} async-done(((bf16[32,64,2,2,128]{4,1,3,2,0:T(8,128)(2,1)}), bf16[32,64,2,2,128]{4,1,3,2,0:T(8,128)(2,1)S(1)}, u32[]{:S(2)}, u32[]{:S(2)}) %all-to-all-start) | async-done | bytes 2097184 | tf_op jit(solution)/shard_map/while/body/eval_jaxpr/all_to_all | solution.py:41
  292.0 6.5 %collective-permute-start = (f32[64,2,2,128]{3,1,0,2:T(2,128)S(1)}, f32[64,2,2,128]{3,1,0,2:T(2,128)S(1)}, u32[]{:S(2)}, u32[]{:S(2)}) collective-permute-start(f32[64,2,2,128]{3,1,0,2:T(2,128)S(1)} %constant_dynamic-update-slice_fusion.5), channel_id=1, source_target_pairs={{0,32},{32,64},{64,96},{96,128},{128,160},{160,192},{192,224},{1,3... | collective-permute-start | bytes 393224 | tf_op jit(solution)/shard_map/while/body/eval_jaxpr/ppermute | solution.py:10
  302.3 5.7 all-to-all-start
  308.1 45.4 %all-to-all-done = bf16[32,64,2,2,128]{4,1,3,2,0:T(8,128)(2,1)S(1)} async-done(((bf16[32,64,2,2,128]{4,1,3,2,0:T(8,128)(2,1)}), bf16[32,64,2,2,128]{4,1,3,2,0:T(8,128)(2,1)S(1)}, u32[]{:S(2)}, u32[]{:S(2)}) %all-to-all-start) | async-done | bytes 2097184 | tf_op jit(solution)/shard_map/while/body/eval_jaxpr/all_to_all | solution.py:41
  364.9 6.5 %collective-permute-start = (f32[64,2,2,128]{3,1,0,2:T(2,128)S(1)}, f32[64,2,2,128]{3,1,0,2:T(2,128)S(1)}, u32[]{:S(2)}, u32[]{:S(2)}) collective-permute-start(f32[64,2,2,128]{3,1,0,2:T(2,128)S(1)} %constant_dynamic-update-slice_fusion.5), channel_id=1, source_target_pairs={{0,32},{32,64},{64,96},{96,128},{128,160},{160,192},{192,224},{1,3... | collective-permute-start | bytes 393224 | tf_op jit(solution)/shard_map/while/body/eval_jaxpr/ppermute | solution.py:10
  375.2 5.7 all-to-all-start
  381.0 45.4 %all-to-all-done = bf16[32,64,2,2,128]{4,1,3,2,0:T(8,128)(2,1)S(1)} async-done(((bf16[32,64,2,2,128]{4,1,3,2,0:T(8,128)(2,1)}), bf16[32,64,2,2,128]{4,1,3,2,0:T(8,128)(2,1)S(1)}, u32[]{:S(2)}, u32[]{:S(2)}) %all-to-all-start) | async-done | bytes 2097184 | tf_op jit(solution)/shard_map/while/body/eval_jaxpr/all_to_all | solution.py:41
  437.8 6.5 %collective-permute-start = (f32[64,2,2,128]{3,1,0,2:T(2,128)S(1)}, f32[64,2,2,128]{3,1,0,2:T(2,128)S(1)}, u32[]{:S(2)}, u32[]{:S(2)}) collective-permute-start(f32[64,2,2,128]{3,1,0,2:T(2,128)S(1)} %constant_dynamic-update-slice_fusion.5), channel_id=1, source_target_pairs={{0,32},{32,64},{64,96},{96,128},{128,160},{160,192},{192,224},{1,3... | collective-permute-start | bytes 393224 | tf_op jit(solution)/shard_map/while/body/eval_jaxpr/ppermute | solution.py:10
  448.1 5.7 all-to-all-start
  453.8 45.4 %all-to-all-done = bf16[32,64,2,2,128]{4,1,3,2,0:T(8,128)(2,1)S(1)} async-done(((bf16[32,64,2,2,128]{4,1,3,2,0:T(8,128)(2,1)}), bf16[32,64,2,2,128]{4,1,3,2,0:T(8,128)(2,1)S(1)}, u32[]{:S(2)}, u32[]{:S(2)}) %all-to-all-start) | async-done | bytes 2097184 | tf_op jit(solution)/shard_map/while/body/eval_jaxpr/all_to_all | solution.py:41
  510.7 6.5 %collective-permute-start = (f32[64,2,2,128]{3,1,0,2:T(2,128)S(1)}, f32[64,2,2,128]{3,1,0,2:T(2,128)S(1)}, u32[]{:S(2)}, u32[]{:S(2)}) collective-permute-start(f32[64,2,2,128]{3,1,0,2:T(2,128)S(1)} %constant_dynamic-update-slice_fusion.5), channel_id=1, source_target_pairs={{0,32},{32,64},{64,96},{96,128},{128,160},{160,192},{192,224},{1,3... | collective-permute-start | bytes 393224 | tf_op jit(solution)/shard_map/while/body/eval_jaxpr/ppermute | solution.py:10
  521.0 5.7 all-to-all-start
  526.7 45.4 %all-to-all-done = bf16[32,64,2,2,128]{4,1,3,2,0:T(8,128)(2,1)S(1)} async-done(((bf16[32,64,2,2,128]{4,1,3,2,0:T(8,128)(2,1)}), bf16[32,64,2,2,128]{4,1,3,2,0:T(8,128)(2,1)S(1)}, u32[]{:S(2)}, u32[]{:S(2)}) %all-to-all-start) | async-done | bytes 2097184 | tf_op jit(solution)/shard_map/while/body/eval_jaxpr/all_to_all | solution.py:41
  583.6 6.5 %collective-permute-start = (f32[64,2,2,128]{3,1,0,2:T(2,128)S(1)}, f32[64,2,2,128]{3,1,0,2:T(2,128)S(1)}, u32[]{:S(2)}, u32[]{:S(2)}) collective-permute-start(f32[64,2,2,128]{3,1,0,2:T(2,128)S(1)} %constant_dynamic-update-slice_fusion.5), channel_id=1, source_target_pairs={{0,32},{32,64},{64,96},{96,128},{128,160},{160,192},{192,224},{1,3... | collective-permute-start | bytes 393224 | tf_op jit(solution)/shard_map/while/body/eval_jaxpr/ppermute | solution.py:10
  607.9 5.0 collective-permute-done.4
  (170 shorter events, 146.3 us)
Async XLA Ops:
  1.7 597.8 %copy-start.2 = (f32[1,2,128]{2,1,0:T(2,128)S(1)}, f32[1,2,128]{2,1,0:T(2,128)}, u32[]{:S(2)}) copy-start(f32[1,2,128]{2,1,0:T(2,128)} %param.8) | copy-start | bytes 3076
  1.7 612.0 %copy-start.1 = (f32[1,64,2,2,128]{4,3,2,1,0:T(2,128)S(1)}, f32[1,64,2,2,128]{4,3,2,1,0:T(2,128)}, u32[]{:S(2)}) copy-start(f32[1,64,2,2,128]{4,3,2,1,0:T(2,128)} %param.6) | copy-start | bytes 393220
  3.7 61.4 %all-to-all-start = ((bf16[32,64,2,2,128]{4,1,3,2,0:T(8,128)(2,1)}), bf16[32,64,2,2,128]{4,1,3,2,0:T(8,128)(2,1)S(1)}, u32[]{:S(2)}, u32[]{:S(2)}) async-start(bf16[32,64,2,2,128]{4,1,3,2,0:T(8,128)(2,1)} %stack.18), calls=%async_computation | async-start | bytes 4194304 | tf_op jit(solution)/shard_map/while/body/eval_jaxpr/all_to_all | solution.py:41
  76.4 5.2 collective-permute-start
  83.6 55.0 %all-to-all-start = ((bf16[32,64,2,2,128]{4,1,3,2,0:T(8,128)(2,1)}), bf16[32,64,2,2,128]{4,1,3,2,0:T(8,128)(2,1)S(1)}, u32[]{:S(2)}, u32[]{:S(2)}) async-start(bf16[32,64,2,2,128]{4,1,3,2,0:T(8,128)(2,1)} %stack.18), calls=%async_computation | async-start | bytes 4194304 | tf_op jit(solution)/shard_map/while/body/eval_jaxpr/all_to_all | solution.py:41
  150.0 5.3 collective-permute-start
  157.2 50.5 %all-to-all-start = ((bf16[32,64,2,2,128]{4,1,3,2,0:T(8,128)(2,1)}), bf16[32,64,2,2,128]{4,1,3,2,0:T(8,128)(2,1)S(1)}, u32[]{:S(2)}, u32[]{:S(2)}) async-start(bf16[32,64,2,2,128]{4,1,3,2,0:T(8,128)(2,1)} %stack.18), calls=%async_computation | async-start | bytes 4194304 | tf_op jit(solution)/shard_map/while/body/eval_jaxpr/all_to_all | solution.py:41
  219.1 8.4 %collective-permute-start = (f32[64,2,2,128]{3,1,0,2:T(2,128)S(1)}, f32[64,2,2,128]{3,1,0,2:T(2,128)S(1)}, u32[]{:S(2)}, u32[]{:S(2)}) collective-permute-start(f32[64,2,2,128]{3,1,0,2:T(2,128)S(1)} %constant_dynamic-update-slice_fusion.5), channel_id=1, source_target_pairs={{0,32},{32,64},{64,96},{96,128},{128,160},{160,192},{192,224},{1,3... | collective-permute-start | bytes 393224 | tf_op jit(solution)/shard_map/while/body/eval_jaxpr/ppermute | solution.py:10
  229.5 51.1 %all-to-all-start = ((bf16[32,64,2,2,128]{4,1,3,2,0:T(8,128)(2,1)}), bf16[32,64,2,2,128]{4,1,3,2,0:T(8,128)(2,1)S(1)}, u32[]{:S(2)}, u32[]{:S(2)}) async-start(bf16[32,64,2,2,128]{4,1,3,2,0:T(8,128)(2,1)} %stack.18), calls=%async_computation | async-start | bytes 4194304 | tf_op jit(solution)/shard_map/while/body/eval_jaxpr/all_to_all | solution.py:41
  292.0 8.4 %collective-permute-start = (f32[64,2,2,128]{3,1,0,2:T(2,128)S(1)}, f32[64,2,2,128]{3,1,0,2:T(2,128)S(1)}, u32[]{:S(2)}, u32[]{:S(2)}) collective-permute-start(f32[64,2,2,128]{3,1,0,2:T(2,128)S(1)} %constant_dynamic-update-slice_fusion.5), channel_id=1, source_target_pairs={{0,32},{32,64},{64,96},{96,128},{128,160},{160,192},{192,224},{1,3... | collective-permute-start | bytes 393224 | tf_op jit(solution)/shard_map/while/body/eval_jaxpr/ppermute | solution.py:10
  302.3 51.1 %all-to-all-start = ((bf16[32,64,2,2,128]{4,1,3,2,0:T(8,128)(2,1)}), bf16[32,64,2,2,128]{4,1,3,2,0:T(8,128)(2,1)S(1)}, u32[]{:S(2)}, u32[]{:S(2)}) async-start(bf16[32,64,2,2,128]{4,1,3,2,0:T(8,128)(2,1)} %stack.18), calls=%async_computation | async-start | bytes 4194304 | tf_op jit(solution)/shard_map/while/body/eval_jaxpr/all_to_all | solution.py:41
  364.9 8.4 %collective-permute-start = (f32[64,2,2,128]{3,1,0,2:T(2,128)S(1)}, f32[64,2,2,128]{3,1,0,2:T(2,128)S(1)}, u32[]{:S(2)}, u32[]{:S(2)}) collective-permute-start(f32[64,2,2,128]{3,1,0,2:T(2,128)S(1)} %constant_dynamic-update-slice_fusion.5), channel_id=1, source_target_pairs={{0,32},{32,64},{64,96},{96,128},{128,160},{160,192},{192,224},{1,3... | collective-permute-start | bytes 393224 | tf_op jit(solution)/shard_map/while/body/eval_jaxpr/ppermute | solution.py:10
  375.2 51.1 %all-to-all-start = ((bf16[32,64,2,2,128]{4,1,3,2,0:T(8,128)(2,1)}), bf16[32,64,2,2,128]{4,1,3,2,0:T(8,128)(2,1)S(1)}, u32[]{:S(2)}, u32[]{:S(2)}) async-start(bf16[32,64,2,2,128]{4,1,3,2,0:T(8,128)(2,1)} %stack.18), calls=%async_computation | async-start | bytes 4194304 | tf_op jit(solution)/shard_map/while/body/eval_jaxpr/all_to_all | solution.py:41
  426.4 3.4 copy-start.3
  437.8 8.4 %collective-permute-start = (f32[64,2,2,128]{3,1,0,2:T(2,128)S(1)}, f32[64,2,2,128]{3,1,0,2:T(2,128)S(1)}, u32[]{:S(2)}, u32[]{:S(2)}) collective-permute-start(f32[64,2,2,128]{3,1,0,2:T(2,128)S(1)} %constant_dynamic-update-slice_fusion.5), channel_id=1, source_target_pairs={{0,32},{32,64},{64,96},{96,128},{128,160},{160,192},{192,224},{1,3... | collective-permute-start | bytes 393224 | tf_op jit(solution)/shard_map/while/body/eval_jaxpr/ppermute | solution.py:10
  448.1 51.1 %all-to-all-start = ((bf16[32,64,2,2,128]{4,1,3,2,0:T(8,128)(2,1)}), bf16[32,64,2,2,128]{4,1,3,2,0:T(8,128)(2,1)S(1)}, u32[]{:S(2)}, u32[]{:S(2)}) async-start(bf16[32,64,2,2,128]{4,1,3,2,0:T(8,128)(2,1)} %stack.18), calls=%async_computation | async-start | bytes 4194304 | tf_op jit(solution)/shard_map/while/body/eval_jaxpr/all_to_all | solution.py:41
  510.7 8.4 %collective-permute-start = (f32[64,2,2,128]{3,1,0,2:T(2,128)S(1)}, f32[64,2,2,128]{3,1,0,2:T(2,128)S(1)}, u32[]{:S(2)}, u32[]{:S(2)}) collective-permute-start(f32[64,2,2,128]{3,1,0,2:T(2,128)S(1)} %constant_dynamic-update-slice_fusion.5), channel_id=1, source_target_pairs={{0,32},{32,64},{64,96},{96,128},{128,160},{160,192},{192,224},{1,3... | collective-permute-start | bytes 393224 | tf_op jit(solution)/shard_map/while/body/eval_jaxpr/ppermute | solution.py:10
  521.0 51.1 %all-to-all-start = ((bf16[32,64,2,2,128]{4,1,3,2,0:T(8,128)(2,1)}), bf16[32,64,2,2,128]{4,1,3,2,0:T(8,128)(2,1)S(1)}, u32[]{:S(2)}, u32[]{:S(2)}) async-start(bf16[32,64,2,2,128]{4,1,3,2,0:T(8,128)(2,1)} %stack.18), calls=%async_computation | async-start | bytes 4194304 | tf_op jit(solution)/shard_map/while/body/eval_jaxpr/all_to_all | solution.py:41
  583.6 8.4 %collective-permute-start = (f32[64,2,2,128]{3,1,0,2:T(2,128)S(1)}, f32[64,2,2,128]{3,1,0,2:T(2,128)S(1)}, u32[]{:S(2)}, u32[]{:S(2)}) collective-permute-start(f32[64,2,2,128]{3,1,0,2:T(2,128)S(1)} %constant_dynamic-update-slice_fusion.5), channel_id=1, source_target_pairs={{0,32},{32,64},{64,96},{96,128},{128,160},{160,192},{192,224},{1,3... | collective-permute-start | bytes 393224 | tf_op jit(solution)/shard_map/while/body/eval_jaxpr/ppermute | solution.py:10
  592.1 22.4 %copy-start = (f32[1,64,2,2,128]{4,3,2,1,0:T(2,128)}, f32[1,64,2,2,128]{4,3,2,1,0:T(2,128)S(1)}, u32[]{:S(2)}) copy-start(f32[1,64,2,2,128]{4,3,2,1,0:T(2,128)S(1)} %get-tuple-element.162) | copy-start | bytes 393220
  592.1 8.1 %collective-permute-start.1 = (bf16[1,64,2,2,128]{4,3,2,1,0:T(2,128)(2,1)S(1)}, bf16[1,64,2,2,128]{4,3,2,1,0:T(2,128)(2,1)S(1)}, u32[]{:S(2)}, u32[]{:S(2)}) collective-permute-start(bf16[1,64,2,2,128]{4,3,2,1,0:T(2,128)(2,1)S(1)} %get-tuple-element.161), channel_id=1, source_target_pairs={{0,32},{32,64},{64,96},{96,128},{128,160},{160,192},{192,224},{1,3... | collective-permute-start | bytes 196616 | tf_op jit(solution)/shard_map/ppermute | solution.py:21
  596.5 5.6 collective-permute-start.2
  602.5 5.4 collective-permute-start.3
  605.4 7.5 %collective-permute-start.4 = (bf16[3,64,1,2,128]{4,3,2,1,0:T(2,128)(2,1)S(1)}, bf16[3,64,1,2,128]{4,3,2,1,0:T(2,128)(2,1)S(1)}, u32[]{:S(2)}, u32[]{:S(2)}) collective-permute-start(bf16[3,64,1,2,128]{4,3,2,1,0:T(2,128)(2,1)S(1)} %get-tuple-element.168), channel_id=1, source_target_pairs={{1,0},{2,1},{3,2},{4,3},{5,4},{6,5},{7,6},{8,7},{9,8},{10,9},{11,1... | collective-permute-start | bytes 294920 | tf_op jit(solution)/shard_map/ppermute | solution.py:23
  (7 other events, 23.7 us)
